TPU v7x, 32 devices: a whole 2x2x4 slice. The times are simulated.
32 devices in a mesh: dp: 2 (over x), row: 4 (over z), col: 4 (over y, core).
Axes of the slice: x: 2, y: 2, z: 4, core: 2. Of those that a mesh axis runs over, the one named last changes fastest.
Arguments:
- layer_input: bfloat16 [1536, 6144], P(('dp', 'col'), 'row'), may hold values from -125 to 125
- grad_output: bfloat16 [1536, 6144], P(('dp', 'col'), 'row'), may hold values from -6 to 6
- pre_activation: bfloat16 [1536, 24576], P(('dp', 'row'), 'col'), may hold values from -6 to 6
- norm_gain_vector: float32 [6144], P('row'), may hold values from 0.5 to 1.5
- up_weight: bfloat16 [6144, 24576], P('row', 'col'), may hold values from -0.078125 to 0.078125
- down_weight: bfloat16 [24576, 6144], P('col', 'row'), may hold values from -0.0390625 to 0.0390625
Outputs:
- input_gradient: float32 [1536, 6144], P(('dp', 'col'), 'row')
- grad_up: float32 [6144, 24576], P(('row', 'dp'), 'col')
- grad_down: float32 [24576, 6144], P('col', ('row', 'dp'))
- grad_bias: float32 [24576], P('col')
- gain_gradient: float32 [6144], P('row')
All inputs are finite; a program needn't handle non-finite values.
Results may differ from a plain program's by a relative error of at most 0.0055.
Values may be sent and summed in bfloat16 or wider, within the bound.
A program may use at most 256 MiB of HBM per device.

v0:
```python
import jax
import jax.numpy as jnp
from jax import lax
from jax.sharding import PartitionSpec as P

CHUNKS = 4
epsilon = 1e-06


def gelu_parts(pre_float):
    normal_cdf = 0.5 * (1.0 + lax.erf(pre_float * 0.7071067811865476))
    normal_pdf = jnp.exp(-0.5 * pre_float * pre_float) * 0.3989422804014327
    return (pre_float * normal_cdf, normal_cdf + pre_float * normal_pdf)


def contract_last(left, right):
    return lax.dot_general(
        left, right, (((1,), (1,)), ((), ())), preferred_element_type=jnp.float32
    )


def contract_first(left, right):
    return lax.dot_general(
        left, right, (((0,), (0,)), ((), ())), preferred_element_type=jnp.float32
    )


def build(sizes):
    swap = [(0, 1), (1, 0)]
    two = sizes["dp"] == 2

    def per_device(
        layer_input, grad_output, pre_activation, norm_gain_vector, up_weight, down_weight
    ):
        model_width = layer_input.shape[1] * sizes["row"]
        hidden = pre_activation.shape[1]
        chunks = CHUNKS if hidden % (CHUNKS * 128) == 0 else 1
        step = hidden // chunks
        me = lax.axis_index("dp")
        grad_all = lax.all_gather(grad_output, "col", axis=0, tiled=True)
        x = layer_input.astype(jnp.float32)
        sum_rows, square_rows = lax.psum((jnp.sum(x, axis=1), jnp.sum(x * x, axis=1)), "row")
        mean = sum_rows / model_width
        inv_std = 1.0 / jnp.sqrt(square_rows / model_width - mean * mean + epsilon)
        xhat = (x - mean[:, None]) * inv_std[:, None]
        normed = (xhat * norm_gain_vector[None, :]).astype(jnp.bfloat16)
        normed_all = lax.all_gather(normed, "col", axis=0, tiled=True)
        half = layer_input.shape[1] // sizes["dp"]

        def part(array, index):
            return lax.dynamic_slice_in_dim(array, index * half, half, axis=1)

        if two:
            normed_mine, normed_other = (part(normed_all, me), part(normed_all, 1 - me))
            grad_mine, grad_other = (part(grad_all, me), part(grad_all, 1 - me))

        def up_of(hid):
            if not two:
                return lax.psum_scatter(
                    contract_first(normed_all, hid), "dp", scatter_dimension=0, tiled=True
                )
            away = contract_first(normed_other, hid).astype(jnp.bfloat16)
            got = lax.ppermute(away, "dp", swap)
            return contract_first(normed_mine, hid) + got.astype(jnp.float32)

        def down_of(act):
            if not two:
                return lax.psum_scatter(
                    contract_first(act, grad_all), "dp", scatter_dimension=1, tiled=True
                )
            away = contract_first(act, grad_other).astype(jnp.bfloat16)
            got = lax.ppermute(away, "dp", swap)
            return contract_first(act, grad_mine) + got.astype(jnp.float32)

        ups, downs, biases, total = ([], [], [], None)
        for k in range(chunks):
            cut = slice(k * step, (k + 1) * step)
            value, slope = gelu_parts(pre_activation[:, cut].astype(jnp.float32))
            grad_act = lax.psum_scatter(
                contract_last(grad_all, down_weight[cut]).astype(jnp.bfloat16),
                "row",
                scatter_dimension=0,
                tiled=True,
            )
            act_all = lax.all_gather(value.astype(jnp.bfloat16), "row", axis=0, tiled=True)
            grad_hidden = (grad_act.astype(jnp.float32) * slope).astype(jnp.bfloat16)
            hid_all = lax.all_gather(grad_hidden, "row", axis=0, tiled=True)
            downs.append(down_of(act_all))
            ups.append(up_of(hid_all))
            biases.append(jnp.sum(hid_all.astype(jnp.float32), axis=0))
            term = contract_last(hid_all, up_weight[:, cut])
            total = term if total is None else total + term
        bias = jnp.concatenate(biases)
        grad_bias = bias + lax.ppermute(bias, "dp", swap) if two else lax.psum(bias, "dp")
        grad_up = jnp.concatenate(ups, axis=1)
        grad_down = jnp.concatenate(downs, axis=0)
        grad_normed = lax.psum_scatter(
            total.astype(jnp.bfloat16), "col", scatter_dimension=0, tiled=True
        ).astype(jnp.float32)
        scaled = grad_normed * norm_gain_vector[None, :]
        first, second = lax.psum((jnp.sum(scaled, axis=1), jnp.sum(scaled * xhat, axis=1)), "row")
        input_gradient = inv_std[:, None] * (
            scaled - first[:, None] / model_width - xhat * (second[:, None] / model_width)
        )
        gain_gradient = lax.psum(jnp.sum(grad_normed * xhat, axis=0), ("dp", "col"))
        return (input_gradient, grad_up, grad_down, grad_bias, gain_gradient)

    return per_device


def solution(mesh):
    placed = (
        P(("dp", "col"), "row"),
        P(("dp", "col"), "row"),
        P(("dp", "row"), "col"),
        P("row"),
        P("row", "col"),
        P("col", "row"),
    )
    return jax.shard_map(
        build(dict(mesh.shape)),
        mesh=mesh,
        in_specs=placed,
        out_specs=(
            P(("dp", "col"), "row"),
            P(("row", "dp"), "col"),
            P("col", ("row", "dp")),
            P("col"),
            P("row"),
        ),
        check_vma=False,
    )
```

profile of v0, /device:TPU:0, one launch (start us, length us, event | category | flops | bytes accessed | tf_op | source)
XLA Modules:
  0.0 974.1 jit_solution(11959575978303377760)
XLA Ops:
  7.9 28.4 %all-gather.11.cloned.1.call-done = bf16[768,1536]{1,0:T(8,128)(2,1)} async-done(((bf16[192,1536]{1,0:T(8,128)(2,1)}), bf16[768,1536]{1,0:T(8,128)(2,1)}) %all-gather.11.cloned.1.call-update) | async-done | bytes 2359312 | tf_op jit(solution)/shard_map/all_gather | solution.py:40
  36.3 8.3 fusion.22
  46.3 7.4 fusion.25
  53.8 7.4 fusion.16
  61.3 7.4 fusion.19
  68.8 23.7 %reduce-scatter.10.cloned.1.call-done = bf16[192,1536]{1,0:T(8,128)(2,1)} async-done(((bf16[768,1536]{1,0:T(8,128)(2,1)}), bf16[192,1536]{1,0:T(8,128)(2,1)}) %reduce-scatter.10.cloned.1.call-update) | async-done | bytes 589840 | tf_op jit(solution)/shard_map/reduce_scatter | solution.py:79
  92.5 50.0 %reduce-scatter.12.cloned.1.call-done = bf16[192,1536]{1,0:T(8,128)(2,1)} async-done(((bf16[768,1536]{1,0:T(8,128)(2,1)}), bf16[192,1536]{1,0:T(8,128)(2,1)}) %reduce-scatter.12.cloned.1.call-update) | async-done | bytes 589840 | tf_op jit(solution)/shard_map/reduce_scatter | solution.py:79
  142.5 49.3 %reduce-scatter.6.cloned.1.call-done = bf16[192,1536]{1,0:T(8,128)(2,1)} async-done(((bf16[768,1536]{1,0:T(8,128)(2,1)}), bf16[192,1536]{1,0:T(8,128)(2,1)}) %reduce-scatter.6.cloned.1.call-update) | async-done | bytes 589840 | tf_op jit(solution)/shard_map/reduce_scatter | solution.py:79
  191.8 49.3 %reduce-scatter.8.cloned.1.call-done = bf16[192,1536]{1,0:T(8,128)(2,1)} async-done(((bf16[768,1536]{1,0:T(8,128)(2,1)}), bf16[192,1536]{1,0:T(8,128)(2,1)}) %reduce-scatter.8.cloned.1.call-update) | async-done | bytes 589840 | tf_op jit(solution)/shard_map/reduce_scatter | solution.py:79
  241.1 5.7 fusion.50
  251.9 44.4 %all-gather.13.cloned.1.call-done = bf16[768,1536]{1,0:T(8,128)(2,1)} async-done(((bf16[192,1536]{1,0:T(8,128)(2,1)}), bf16[768,1536]{1,0:T(8,128)(2,1)}) %all-gather.13.cloned.1.call-update) | async-done | bytes 2359312 | tf_op jit(solution)/shard_map/all_gather | solution.py:87
  296.3 9.1 fusion.12
  305.4 41.8 %all-gather.17.cloned.1.call-done = bf16[768,1536]{1,0:T(8,128)(2,1)} async-done(((bf16[192,1536]{1,0:T(8,128)(2,1)}), bf16[768,1536]{1,0:T(8,128)(2,1)}) %all-gather.17.cloned.1.call-update) | async-done | bytes 2359312 | tf_op jit(solution)/shard_map/all_gather | solution.py:87
  347.3 9.1 fusion.4
  356.3 41.3 %all-gather.15.cloned.1.call-done = bf16[768,1536]{1,0:T(8,128)(2,1)} async-done(((bf16[192,1536]{1,0:T(8,128)(2,1)}), bf16[768,1536]{1,0:T(8,128)(2,1)}) %all-gather.15.cloned.1.call-update) | async-done | bytes 2359312 | tf_op jit(solution)/shard_map/all_gather | solution.py:87
  397.6 9.0 fusion.8
  406.6 41.3 %all-gather.19.cloned.1.call-done = bf16[768,1536]{1,0:T(8,128)(2,1)} async-done(((bf16[192,1536]{1,0:T(8,128)(2,1)}), bf16[768,1536]{1,0:T(8,128)(2,1)}) %all-gather.19.cloned.1.call-update) | async-done | bytes 2359312 | tf_op jit(solution)/shard_map/all_gather | solution.py:87
  447.9 12.6 %add_convert_fusion = bf16[768,1536]{1,0:T(8,128)(2,1)} fusion(f32[768,1536]{1,0:T(8,128)} %fusion.4, f32[768,1536]{1,0:T(8,128)} %fusion.12, f32[768,1536]{1,0:T(8,128)} %fusion.8, bf16[768,1536]{1,0:T(8,128)(2,1)} %all-gather.19.cloned.1.call-done, bf16[1536,6144]{1,0:T(8,128)(2,1)} %param.10), kind=kOutput, calls=%fused_computation.14 | convolution fusion | flops 3628597248 | bytes 23592960 | tf_op jit(solution)/shard_map/dot_general | solution.py:17
  461.9 10.4 %all-reduce.1 = (f32[192]{0:T(256)S(1)}, f32[192]{0:T(256)S(1)}) all-reduce(f32[192]{0:T(256)S(1)} %get-tuple-element.9, f32[192]{0:T(256)S(1)} %get-tuple-element.8), channel_id=1, replica_groups=mesh['dp'=2,'row'=4,'col'=4] {'row'}, use_global_device_ids=true, to_apply=%region_3.0 | all-reduce | flops 384 | bytes 3072 | tf_op jit(solution)/shard_map/psum | solution.py:42
  472.3 26.1 %all-gather.29.cloned.1.call-done = bf16[768,1536]{1,0:T(8,128)(2,1)} async-done(((bf16[192,1536]{1,0:T(8,128)(2,1)}), bf16[768,1536]{1,0:T(8,128)(2,1)}) %all-gather.29.cloned.1.call-update) | async-done | bytes 2359312 | tf_op jit(solution)/shard_map/all_gather | solution.py:85
  498.4 5.1 convolution_convert_fusion
  505.0 43.8 %all-gather.27.cloned.1.call-done = bf16[768,1536]{1,0:T(8,128)(2,1)} async-done(((bf16[192,1536]{1,0:T(8,128)(2,1)}), bf16[768,1536]{1,0:T(8,128)(2,1)}) %all-gather.27.cloned.1.call-update) | async-done | bytes 2359312 | tf_op jit(solution)/shard_map/all_gather | solution.py:85
  548.8 5.1 convolution_convert_fusion.1
  555.3 43.6 %all-gather.25.cloned.1.call-done = bf16[768,1536]{1,0:T(8,128)(2,1)} async-done(((bf16[192,1536]{1,0:T(8,128)(2,1)}), bf16[768,1536]{1,0:T(8,128)(2,1)}) %all-gather.25.cloned.1.call-update) | async-done | bytes 2359312 | tf_op jit(solution)/shard_map/all_gather | solution.py:85
  599.0 5.2 convolution_convert_fusion.2
  605.6 44.3 %all-gather.23.cloned.1.call-done = bf16[768,1536]{1,0:T(8,128)(2,1)} async-done(((bf16[192,1536]{1,0:T(8,128)(2,1)}), bf16[768,1536]{1,0:T(8,128)(2,1)}) %all-gather.23.cloned.1.call-update) | async-done | bytes 2359312 | tf_op jit(solution)/shard_map/all_gather | solution.py:85
  649.9 5.1 convolution_convert_fusion.3
  656.4 27.5 %reduce-scatter.14.cloned.1.call-done = bf16[192,1536]{1,0:T(8,128)(2,1)} async-done(((bf16[768,1536]{1,0:T(8,128)(2,1)}), bf16[192,1536]{1,0:T(8,128)(2,1)}) %reduce-scatter.14.cloned.1.call-update) | async-done | bytes 589840 | tf_op jit(solution)/shard_map/reduce_scatter | solution.py:97
  683.9 2.6 fusion.36
  686.5 2.2 convert_reduce_fusion
  692.3 16.4 %collective-permute-done.8 = f32[6144]{0:T(1024)S(1)} collective-permute-done((f32[6144]{0:T(1024)S(1)}, f32[6144]{0:T(1024)S(1)}, u32[]{:S(2)}, u32[]{:S(2)}) %collective-permute-start.8) | collective-permute-done | bytes 24608 | tf_op jit(solution)/shard_map/ppermute | solution.py:94
  709.4 7.6 convert_add_fusion
  717.0 6.0 convert_add_fusion.1
  723.1 6.0 convert_add_fusion.2
  729.1 5.9 convert_add_fusion.3
  734.9 5.6 convolution_convert_fusion.7
  742.1 3.4 convolution_convert_fusion.6
  746.0 3.5 convolution_convert_fusion.5
  751.3 6.8 pad_maximum_fusion.1
  758.1 9.7 all-reduce
  767.8 135.6 %psum.39 = f32[1536]{0:T(1024)} all-reduce(f32[1536]{0:T(1024)S(1)} %get-tuple-element.5), channel_id=1, replica_groups=mesh['dp'=2,'row'=4,'col'=4] {'dp','col'}, use_global_device_ids=true, to_apply=%region_18.0 | all-reduce | flops 1536 | bytes 12288 | tf_op jit(solution)/shard_map/psum | solution.py:105
  903.4 4.2 convolution_convert_fusion.4
  909.7 4.0 convert_add_fusion.7
  913.7 3.8 convert_add_fusion.6
  917.5 4.0 convert_add_fusion.5
  921.5 36.5 %collective-permute-done.3 = bf16[768,1536]{1,0:T(8,128)(2,1)S(1)} collective-permute-done((bf16[768,1536]{1,0:T(8,128)(2,1)S(1)}, bf16[768,1536]{1,0:T(8,128)(2,1)S(1)}, u32[]{:S(2)}, u32[]{:S(2)}) %collective-permute-start.3) | collective-permute-done | bytes 2359328 | tf_op jit(solution)/shard_map/ppermute | solution.py:63
  958.0 2.1 convert_add_fusion.4
  960.1 7.3 pad_maximum_fusion
  (114 shorter events, 24.8 us)
Async XLA Ops:
  7.2 29.2 %all-gather.11.cloned.1.call-start = ((), (), s32[]{:S(2)}) async-start(), calls=%async_computation.5 | async-start | bytes 2949120 | tf_op jit(solution)/shard_map/all_gather | solution.py:40
  7.9 84.6 %reduce-scatter.10.cloned.1.call-start = ((), (), s32[]{:S(2)}) async-start(), calls=%async_computation.10 | async-start | bytes 2949120 | tf_op jit(solution)/shard_map/reduce_scatter | solution.py:79
  44.7 97.9 %reduce-scatter.12.cloned.1.call-start = ((), (), s32[]{:S(2)}) async-start(), calls=%async_computation.12 | async-start | bytes 2949120 | tf_op jit(solution)/shard_map/reduce_scatter | solution.py:79
  53.7 138.1 %reduce-scatter.6.cloned.1.call-start = ((), (), s32[]{:S(2)}) async-start(), calls=%async_computation.6 | async-start | bytes 2949120 | tf_op jit(solution)/shard_map/reduce_scatter | solution.py:79
  61.3 179.8 %reduce-scatter.8.cloned.1.call-start = ((), (), s32[]{:S(2)}) async-start(), calls=%async_computation.8 | async-start | bytes 2949120 | tf_op jit(solution)/shard_map/reduce_scatter | solution.py:79
  68.7 172.4 %copy-start.9 = (bf16[192,6144]{1,0:T(8,128)(2,1)S(1)}, bf16[192,6144]{1,0:T(8,128)(2,1)}, u32[]{:S(2)}) copy-start(bf16[192,6144]{1,0:T(8,128)(2,1)} %param.8) | copy-start | bytes 7077892
  68.8 227.6 %all-gather.13.cloned.1.call-start = ((), (), s32[]{:S(2)}) async-start(), calls=%async_computation.7 | async-start | bytes 2949120 | tf_op jit(solution)/shard_map/all_gather | solution.py:87
  246.8 100.4 %all-gather.17.cloned.1.call-start = ((), (), s32[]{:S(2)}) async-start(), calls=%async_computation.11 | async-start | bytes 2949120 | tf_op jit(solution)/shard_map/all_gather | solution.py:87
  247.6 150.0 %all-gather.15.cloned.1.call-start = ((), (), s32[]{:S(2)}) async-start(), calls=%async_computation.9 | async-start | bytes 2949120 | tf_op jit(solution)/shard_map/all_gather | solution.py:87
  248.3 199.6 %all-gather.19.cloned.1.call-start = ((), (), s32[]{:S(2)}) async-start(), calls=%async_computation.13 | async-start | bytes 2949120 | tf_op jit(solution)/shard_map/all_gather | solution.py:87
  249.1 249.3 %all-gather.29.cloned.1.call-start = ((), (), s32[]{:S(2)}) async-start(), calls=%async_computation.19 | async-start | bytes 2949120 | tf_op jit(solution)/shard_map/all_gather | solution.py:85
  249.6 299.1 %all-gather.27.cloned.1.call-start = ((), (), s32[]{:S(2)}) async-start(), calls=%async_computation.18 | async-start | bytes 2949120 | tf_op jit(solution)/shard_map/all_gather | solution.py:85
  250.4 348.6 %all-gather.25.cloned.1.call-start = ((), (), s32[]{:S(2)}) async-start(), calls=%async_computation.17 | async-start | bytes 2949120 | tf_op jit(solution)/shard_map/all_gather | solution.py:85
  251.0 398.9 %all-gather.23.cloned.1.call-start = ((), (), s32[]{:S(2)}) async-start(), calls=%async_computation.16 | async-start | bytes 2949120 | tf_op jit(solution)/shard_map/all_gather | solution.py:85
  251.7 432.2 %reduce-scatter.14.cloned.1.call-start = ((), (), s32[]{:S(2)}) async-start(), calls=%async_computation.14 | async-start | bytes 2949120 | tf_op jit(solution)/shard_map/reduce_scatter | solution.py:97
  460.6 37.9 %copy-start.12 = (bf16[768,1536]{1,0:T(8,128)(2,1)S(1)}, bf16[768,1536]{1,0:T(8,128)(2,1)}, u32[]{:S(2)}) copy-start(bf16[768,1536]{1,0:T(8,128)(2,1)} %all-gather.11.cloned.1.call-done) | copy-start | bytes 7077892
  460.6 274.4 %all-gather.21.cloned.1.call-start = ((), (), s32[]{:S(2)}) async-start(), calls=%async_computation.15 | async-start | bytes 2949120 | tf_op jit(solution)/shard_map/all_gather | solution.py:47
  503.5 205.9 %collective-permute-start.7 = (bf16[1536,768]{1,0:T(8,128)(2,1)}, bf16[1536,768]{1,0:T(8,128)(2,1)}, u32[]{:S(2)}, u32[]{:S(2)}) collective-permute-start(bf16[1536,768]{1,0:T(8,128)(2,1)} %convolution_convert_fusion), channel_id=1, source_target_pairs={{0,16},{16,0},{1,17},{17,1},{2,18},{18,2},{3,19},{19,3},{4,20},{20... | collective-permute-start | bytes 7077896 | tf_op jit(solution)/shard_map/ppermute | solution.py:72
  553.9 163.1 %collective-permute-start.6 = (bf16[1536,768]{1,0:T(8,128)(2,1)}, bf16[1536,768]{1,0:T(8,128)(2,1)}, u32[]{:S(2)}, u32[]{:S(2)}) collective-permute-start(bf16[1536,768]{1,0:T(8,128)(2,1)} %convolution_convert_fusion.1), channel_id=1, source_target_pairs={{0,16},{16,0},{1,17},{17,1},{2,18},{18,2},{3,19},{19,3},{4,20},{20... | collective-permute-start | bytes 7077896 | tf_op jit(solution)/shard_map/ppermute | solution.py:72
  604.1 79.8 %copy-start.10 = (f32[1536]{0:T(1024)S(1)}, f32[1536]{0:T(1024)}, u32[]{:S(2)}) copy-start(f32[1536]{0:T(1024)} %param.9) | copy-start | bytes 18436
  604.1 118.9 %collective-permute-start.5 = (bf16[1536,768]{1,0:T(8,128)(2,1)}, bf16[1536,768]{1,0:T(8,128)(2,1)}, u32[]{:S(2)}, u32[]{:S(2)}) collective-permute-start(bf16[1536,768]{1,0:T(8,128)(2,1)} %convolution_convert_fusion.2), channel_id=1, source_target_pairs={{0,16},{16,0},{1,17},{17,1},{2,18},{18,2},{3,19},{19,3},{4,20},{20... | collective-permute-start | bytes 7077896 | tf_op jit(solution)/shard_map/ppermute | solution.py:72
  655.0 74.1 %collective-permute-start.4 = (bf16[1536,768]{1,0:T(8,128)(2,1)}, bf16[1536,768]{1,0:T(8,128)(2,1)}, u32[]{:S(2)}, u32[]{:S(2)}) collective-permute-start(bf16[1536,768]{1,0:T(8,128)(2,1)} %convolution_convert_fusion.3), channel_id=1, source_target_pairs={{0,16},{16,0},{1,17},{17,1},{2,18},{18,2},{3,19},{19,3},{4,20},{20... | collective-permute-start | bytes 7077896 | tf_op jit(solution)/shard_map/ppermute | solution.py:72
  683.9 4.8 copy-start.1
  686.5 2.6 copy-start.5
  690.8 18.0 %collective-permute-start.8 = (f32[6144]{0:T(1024)S(1)}, f32[6144]{0:T(1024)S(1)}, u32[]{:S(2)}, u32[]{:S(2)}) collective-permute-start(f32[6144]{0:T(1024)S(1)} %pad_maximum_fusion.2), channel_id=1, source_target_pairs={{0,16},{16,0},{1,17},{17,1},{2,18},{18,2},{3,19},{19,3},{4,20},{20... | collective-permute-start | bytes 73736 | tf_op jit(solution)/shard_map/ppermute | solution.py:94
  709.4 7.6 copy-start.13
  709.4 7.6 copy-start.14
  717.0 6.1 copy-start.15
  723.0 6.0 copy-start.16
  734.9 7.1 copy-start.6
  734.9 7.1 copy-start.17
  734.9 16.3 %slice-start.6 = ((s8[4718592]{0:T(1024)(128)(4,1)}), s8[4194304]{0:T(1024)(128)(4,1)S(1)}, s32[]{:S(2)}) async-start(s8[4718592]{0:T(1024)(128)(4,1)} %bitcast.30), calls=%async_computation.26 | async-start | bytes 8388608
  740.5 10.7 %slice-start.7 = ((s8[4718592]{0:T(1024)(128)(4,1)}), s8[524288]{0:T(1024)(128)(4,1)S(1)}, s32[]{:S(2)}) async-start(s8[4718592]{0:T(1024)(128)(4,1)} %bitcast.30), calls=%async_computation.27 | async-start | bytes 1048576
  740.5 169.2 %collective-permute-start = (bf16[768,1536]{1,0:T(8,128)(2,1)}, bf16[768,1536]{1,0:T(8,128)(2,1)}, u32[]{:S(2)}, u32[]{:S(2)}) collective-permute-start(bf16[768,1536]{1,0:T(8,128)(2,1)} %convolution_convert_fusion.7), channel_id=1, source_target_pairs={{0,16},{16,0},{1,17},{17,1},{2,18},{18,2},{3,19},{19,3},{4,20},{20... | collective-permute-start | bytes 7077896 | tf_op jit(solution)/shard_map/ppermute | solution.py:63
  742.0 9.2 slice-start
  742.0 9.2 slice-start.2
  742.1 9.2 slice-start.4
  745.5 5.7 slice-start.1
  745.5 5.7 slice-start.3
  745.5 5.7 slice-start.5
  745.5 168.1 %collective-permute-start.1 = (bf16[768,1536]{1,0:T(8,128)(2,1)}, bf16[768,1536]{1,0:T(8,128)(2,1)}, u32[]{:S(2)}, u32[]{:S(2)}) collective-permute-start(bf16[768,1536]{1,0:T(8,128)(2,1)} %convolution_convert_fusion.6), channel_id=1, source_target_pairs={{0,16},{16,0},{1,17},{17,1},{2,18},{18,2},{3,19},{19,3},{4,20},{20... | collective-permute-start | bytes 7077896 | tf_op jit(solution)/shard_map/ppermute | solution.py:63
  749.5 168.0 %collective-permute-start.2 = (bf16[768,1536]{1,0:T(8,128)(2,1)}, bf16[768,1536]{1,0:T(8,128)(2,1)}, u32[]{:S(2)}, u32[]{:S(2)}) collective-permute-start(bf16[768,1536]{1,0:T(8,128)(2,1)} %convolution_convert_fusion.5), channel_id=1, source_target_pairs={{0,16},{16,0},{1,17},{17,1},{2,18},{18,2},{3,19},{19,3},{4,20},{20... | collective-permute-start | bytes 7077896 | tf_op jit(solution)/shard_map/ppermute | solution.py:63
  903.4 4.8 copy-start.8
  903.4 6.3 copy-start.18
  907.6 2.1 copy-start.3
  907.6 50.4 %collective-permute-start.3 = (bf16[768,1536]{1,0:T(8,128)(2,1)S(1)}, bf16[768,1536]{1,0:T(8,128)(2,1)S(1)}, u32[]{:S(2)}, u32[]{:S(2)}) collective-permute-start(bf16[768,1536]{1,0:T(8,128)(2,1)S(1)} %convolution_convert_fusion.4), channel_id=1, source_target_pairs={{0,16},{16,0},{1,17},{17,1},{2,18},{18,2},{3,19},{19,3},{4,20},{20... | collective-permute-start | bytes 7077896 | tf_op jit(solution)/shard_map/ppermute | solution.py:63
  909.7 4.0 copy-start.7
  917.5 40.5 %copy-start.4 = (bf16[768,1536]{1,0:T(8,128)(2,1)S(1)}, bf16[768,1536]{1,0:T(8,128)(2,1)}, u32[]{:S(2)}) copy-start(bf16[768,1536]{1,0:T(8,128)(2,1)} %all-gather.19.cloned.1.call-done) | copy-start | bytes 7077892
  (3 other events, 4.4 us)
Sparse Core Ops, SparseCore 0:
  9.5 26.7 all-gather.10
  44.8 47.6 reduce-scatter.9
  95.4 47.0 reduce-scatter.11
  144.7 47.0 reduce-scatter.5
  194.0 47.0 reduce-scatter.7
  246.9 49.3 all-gather.12
  298.5 48.7 all-gather.16
  348.8 48.7 all-gather.14
  399.2 48.7 all-gather.18
  449.4 48.9 all-gather.28
  500.0 48.7 all-gather.26
  550.2 48.7 all-gather.24
  601.1 48.7 all-gather.22
  652.3 31.5 reduce-scatter.13
  686.6 24.0 all-gather.20
where the time goes:
time: 981 us; the launch traced here: 974 us
  waiting for transfers between devices  613 us (62%)
  blocking collectives  156 us (16%)
  matrix products  147 us (15%)
  other arithmetic  28.1 us (3%)
  between operations  14.4 us (1%)
  starting transfers between devices  12.4 us (1%)
    reduce_scatter x4, waiting for transfers between devices, per_device(): lax.psum_scatter(contract_last(grad_all, down_weight[cut]).astype(jnp.bfl...  172 us
    all_gather x4, waiting for transfers between devices, per_device(): hid_all = lax.all_gather(grad_hidden, 'row', axis=0, tiled=True)  169 us
    all_gather x4, waiting for transfers between devices, per_device(): lax.all_gather(value.astype(jnp.bfloat16), 'row', axis=0, tiled=True)  158 us
    psum x1, blocking collectives, per_device(): gain_gradient = lax.psum(jnp.sum(grad_normed * xhat, axis=0), ('dp', 'col'))  136 us
    dot_general x16, matrix products, contract_first(): lax.dot_general(left, right, (((0,), (0,)), ((), ())), preferred_element_...  76.5 us
    dot_general x8, matrix products, contract_last(): lax.dot_general(left, right, (((1,), (1,)), ((), ())), preferred_element_...  70.4 us
    ppermute x4, waiting for transfers between devices, up_of(): got = lax.ppermute(away, 'dp', swap)  36.6 us
    all_gather x1, waiting for transfers between devices, per_device(): grad_all = lax.all_gather(grad_output, 'col', axis=0, tiled=True)  28.4 us
  transfers between devices with their start and end apart: 24, of which 16 were waited for; matrix products, arithmetic and copies ran while one was open for 15% of the time, Pallas kernels for 0%

commit v1 on v0

--- a/solution.py
+++ b/solution.py
@@ -102,7 +102,9 @@
         input_gradient = inv_std[:, None] * (
             scaled - first[:, None] / model_width - xhat * (second[:, None] / model_width)
         )
-        gain_gradient = lax.psum(jnp.sum(grad_normed * xhat, axis=0), ("dp", "col"))
+        block = jnp.sum(grad_normed * xhat, axis=0)
+        parts = lax.all_gather(block, ("dp", "col"))
+        gain_gradient = jnp.sum(parts, axis=0)
         return (input_gradient, grad_up, grad_down, grad_bias, gain_gradient)
 
     return per_device

time: 981 us -> 988 us (level)
    all_gather x0 -> x1, blocking collectives: none -> 138 us  [per_device(): parts = lax.all_gather(block, ('dp', 'col'))]
    psum x1 -> x0, blocking collectives: 136 us -> none  [per_device(): gain_gradient = lax.psum(jnp.sum(grad_normed * xhat, axis=0), ('dp', 'col'))]
where the time goes in v1:
time: 988 us; the launch traced here: 981 us
  waiting for transfers between devices  613 us (62%)
  blocking collectives  159 us (16%)
  matrix products  149 us (15%)
  other arithmetic  28.9 us (3%)
  between operations  14.4 us (1%)
  starting transfers between devices  13.1 us (1%)
    reduce_scatter x4, waiting for transfers between devices, per_device(): lax.psum_scatter(contract_last(grad_all, down_weight[cut]).astype(jnp.bfl...  172 us
    all_gather x4, waiting for transfers between devices, per_device(): hid_all = lax.all_gather(grad_hidden, 'row', axis=0, tiled=True)  169 us
    all_gather x4, waiting for transfers between devices, per_device(): lax.all_gather(value.astype(jnp.bfloat16), 'row', axis=0, tiled=True)  158 us
    all_gather x1, blocking collectives, per_device(): parts = lax.all_gather(block, ('dp', 'col'))  138 us
    dot_general x16, matrix products, contract_first(): lax.dot_general(left, right, (((0,), (0,)), ((), ())), preferred_element_...  78.7 us
    dot_general x8, matrix products, contract_last(): lax.dot_general(left, right, (((1,), (1,)), ((), ())), preferred_element_...  70.3 us
    ppermute x4, waiting for transfers between devices, up_of(): got = lax.ppermute(away, 'dp', swap)  36.8 us
    all_gather x1, waiting for transfers between devices, per_device(): grad_all = lax.all_gather(grad_output, 'col', axis=0, tiled=True)  28.4 us
  transfers between devices with their start and end apart: 24, of which 16 were waited for; matrix products, arithmetic and copies ran while one was open for 15% of the time, Pallas kernels for 0%

profile of v1, /device:TPU:0, one launch (start us, length us, event | category | flops | bytes accessed | tf_op | source)
XLA Modules:
  0.0 981.1 jit_solution(17479378747184636288)
XLA Ops:
  7.9 28.4 %all-gather.13.cloned.1.call-done = bf16[768,1536]{1,0:T(8,128)(2,1)} async-done(((bf16[192,1536]{1,0:T(8,128)(2,1)}), bf16[768,1536]{1,0:T(8,128)(2,1)}) %all-gather.13.cloned.1.call-update) | async-done | bytes 2359312 | tf_op jit(solution)/shard_map/all_gather | solution.py:40
  36.3 8.3 fusion.22
  46.3 7.4 fusion.25
  53.8 7.4 fusion.16
  61.3 7.4 fusion.19
  68.8 23.8 %reduce-scatter.10.cloned.1.call-done = bf16[192,1536]{1,0:T(8,128)(2,1)} async-done(((bf16[768,1536]{1,0:T(8,128)(2,1)}), bf16[192,1536]{1,0:T(8,128)(2,1)}) %reduce-scatter.10.cloned.1.call-update) | async-done | bytes 589840 | tf_op jit(solution)/shard_map/reduce_scatter | solution.py:79
  92.5 50.0 %reduce-scatter.12.cloned.1.call-done = bf16[192,1536]{1,0:T(8,128)(2,1)} async-done(((bf16[768,1536]{1,0:T(8,128)(2,1)}), bf16[192,1536]{1,0:T(8,128)(2,1)}) %reduce-scatter.12.cloned.1.call-update) | async-done | bytes 589840 | tf_op jit(solution)/shard_map/reduce_scatter | solution.py:79
  142.5 49.3 %reduce-scatter.6.cloned.1.call-done = bf16[192,1536]{1,0:T(8,128)(2,1)} async-done(((bf16[768,1536]{1,0:T(8,128)(2,1)}), bf16[192,1536]{1,0:T(8,128)(2,1)}) %reduce-scatter.6.cloned.1.call-update) | async-done | bytes 589840 | tf_op jit(solution)/shard_map/reduce_scatter | solution.py:79
  191.8 49.2 %reduce-scatter.8.cloned.1.call-done = bf16[192,1536]{1,0:T(8,128)(2,1)} async-done(((bf16[768,1536]{1,0:T(8,128)(2,1)}), bf16[192,1536]{1,0:T(8,128)(2,1)}) %reduce-scatter.8.cloned.1.call-update) | async-done | bytes 589840 | tf_op jit(solution)/shard_map/reduce_scatter | solution.py:79
  241.1 5.7 fusion.50
  251.9 44.4 %all-gather.15.cloned.1.call-done = bf16[768,1536]{1,0:T(8,128)(2,1)} async-done(((bf16[192,1536]{1,0:T(8,128)(2,1)}), bf16[768,1536]{1,0:T(8,128)(2,1)}) %all-gather.15.cloned.1.call-update) | async-done | bytes 2359312 | tf_op jit(solution)/shard_map/all_gather | solution.py:87
  296.3 9.1 fusion.12
  305.4 41.8 %all-gather.19.cloned.1.call-done = bf16[768,1536]{1,0:T(8,128)(2,1)} async-done(((bf16[192,1536]{1,0:T(8,128)(2,1)}), bf16[768,1536]{1,0:T(8,128)(2,1)}) %all-gather.19.cloned.1.call-update) | async-done | bytes 2359312 | tf_op jit(solution)/shard_map/all_gather | solution.py:87
  347.2 9.1 fusion.4
  356.3 41.3 %all-gather.17.cloned.1.call-done = bf16[768,1536]{1,0:T(8,128)(2,1)} async-done(((bf16[192,1536]{1,0:T(8,128)(2,1)}), bf16[768,1536]{1,0:T(8,128)(2,1)}) %all-gather.17.cloned.1.call-update) | async-done | bytes 2359312 | tf_op jit(solution)/shard_map/all_gather | solution.py:87
  397.6 9.0 fusion.8
  406.6 41.3 %all-gather.21.cloned.1.call-done = bf16[768,1536]{1,0:T(8,128)(2,1)} async-done(((bf16[192,1536]{1,0:T(8,128)(2,1)}), bf16[768,1536]{1,0:T(8,128)(2,1)}) %all-gather.21.cloned.1.call-update) | async-done | bytes 2359312 | tf_op jit(solution)/shard_map/all_gather | solution.py:87
  447.9 12.6 %add_convert_fusion = bf16[768,1536]{1,0:T(8,128)(2,1)} fusion(f32[768,1536]{1,0:T(8,128)} %fusion.4, f32[768,1536]{1,0:T(8,128)} %fusion.12, f32[768,1536]{1,0:T(8,128)} %fusion.8, bf16[768,1536]{1,0:T(8,128)(2,1)} %all-gather.21.cloned.1.call-done, bf16[1536,6144]{1,0:T(8,128)(2,1)} %param.10), kind=kOutput, calls=%fused_computation.14 | convolution fusion | flops 3628597248 | bytes 23592960 | tf_op jit(solution)/shard_map/dot_general | solution.py:17
  461.8 10.4 %all-reduce.1 = (f32[192]{0:T(256)S(1)}, f32[192]{0:T(256)S(1)}) all-reduce(f32[192]{0:T(256)S(1)} %get-tuple-element.9, f32[192]{0:T(256)S(1)} %get-tuple-element.8), channel_id=1, replica_groups=mesh['dp'=2,'row'=4,'col'=4] {'row'}, use_global_device_ids=true, to_apply=%region_3.0 | all-reduce | flops 384 | bytes 3072 | tf_op jit(solution)/shard_map/psum | solution.py:42
  472.3 26.1 %all-gather.31.cloned.1.call-done = bf16[768,1536]{1,0:T(8,128)(2,1)} async-done(((bf16[192,1536]{1,0:T(8,128)(2,1)}), bf16[768,1536]{1,0:T(8,128)(2,1)}) %all-gather.31.cloned.1.call-update) | async-done | bytes 2359312 | tf_op jit(solution)/shard_map/all_gather | solution.py:85
  498.4 5.1 convolution_convert_fusion
  505.0 43.8 %all-gather.29.cloned.1.call-done = bf16[768,1536]{1,0:T(8,128)(2,1)} async-done(((bf16[192,1536]{1,0:T(8,128)(2,1)}), bf16[768,1536]{1,0:T(8,128)(2,1)}) %all-gather.29.cloned.1.call-update) | async-done | bytes 2359312 | tf_op jit(solution)/shard_map/all_gather | solution.py:85
  548.8 5.1 convolution_convert_fusion.1
  555.3 43.6 %all-gather.27.cloned.1.call-done = bf16[768,1536]{1,0:T(8,128)(2,1)} async-done(((bf16[192,1536]{1,0:T(8,128)(2,1)}), bf16[768,1536]{1,0:T(8,128)(2,1)}) %all-gather.27.cloned.1.call-update) | async-done | bytes 2359312 | tf_op jit(solution)/shard_map/all_gather | solution.py:85
  599.0 5.2 convolution_convert_fusion.2
  605.6 44.3 %all-gather.25.cloned.1.call-done = bf16[768,1536]{1,0:T(8,128)(2,1)} async-done(((bf16[192,1536]{1,0:T(8,128)(2,1)}), bf16[768,1536]{1,0:T(8,128)(2,1)}) %all-gather.25.cloned.1.call-update) | async-done | bytes 2359312 | tf_op jit(solution)/shard_map/all_gather | solution.py:85
  649.9 5.1 convolution_convert_fusion.3
  656.4 27.4 %reduce-scatter.14.cloned.1.call-done = bf16[192,1536]{1,0:T(8,128)(2,1)} async-done(((bf16[768,1536]{1,0:T(8,128)(2,1)}), bf16[192,1536]{1,0:T(8,128)(2,1)}) %reduce-scatter.14.cloned.1.call-update) | async-done | bytes 589840 | tf_op jit(solution)/shard_map/reduce_scatter | solution.py:97
  683.9 2.6 fusion.36
  686.5 2.2 convert_reduce_fusion
  692.3 16.4 %collective-permute-done.8 = f32[6144]{0:T(1024)S(1)} collective-permute-done((f32[6144]{0:T(1024)S(1)}, f32[6144]{0:T(1024)S(1)}, u32[]{:S(2)}, u32[]{:S(2)}) %collective-permute-start.8) | collective-permute-done | bytes 24608 | tf_op jit(solution)/shard_map/ppermute | solution.py:94
  709.4 7.6 convert_add_fusion
  717.0 6.0 convert_add_fusion.1
  723.1 6.0 convert_add_fusion.2
  729.1 5.9 convert_add_fusion.3
  734.9 5.6 convolution_convert_fusion.7
  742.1 5.6 convolution_convert_fusion.6
  748.3 7.0 pad_maximum_fusion.1
  755.3 3.4 convolution_convert_fusion.5
  760.3 138.3 %all-gather.1 = f32[8,1,1536]{2,1,0:T(1,128)S(1)} all-gather(f32[1,1,1536]{2,1,0:T(1,128)S(1)} %reshape.18), channel_id=2, replica_groups=mesh['dp'=2,'row'=4,'col'=4] {'dp','col'}, dimensions={0}, use_global_device_ids=true | all-gather | bytes 55296 | tf_op jit(solution)/shard_map/all_gather | solution.py:106
  899.3 9.9 %all-reduce = (f32[192]{0:T(256)S(1)}, f32[192]{0:T(256)S(1)}) all-reduce(f32[192]{0:T(256)S(1)} %get-tuple-element.6, f32[192]{0:T(256)S(1)} %get-tuple-element.7), channel_id=1, replica_groups=mesh['dp'=2,'row'=4,'col'=4] {'row'}, use_global_device_ids=true, to_apply=%region_12.0 | all-reduce | flops 384 | bytes 3072 | tf_op jit(solution)/shard_map/psum | solution.py:101
  909.2 4.2 convolution_convert_fusion.4
  916.4 4.0 convert_add_fusion.7
  920.4 3.8 convert_add_fusion.6
  924.2 4.0 convert_add_fusion.5
  928.1 36.8 %collective-permute-done.3 = bf16[768,1536]{1,0:T(8,128)(2,1)S(1)} collective-permute-done((bf16[768,1536]{1,0:T(8,128)(2,1)S(1)}, bf16[768,1536]{1,0:T(8,128)(2,1)S(1)}, u32[]{:S(2)}, u32[]{:S(2)}) %collective-permute-start.3) | collective-permute-done | bytes 2359328 | tf_op jit(solution)/shard_map/ppermute | solution.py:63
  965.0 2.1 convert_add_fusion.4
  967.0 7.3 pad_maximum_fusion
  (111 shorter events, 26.1 us)
Async XLA Ops:
  7.2 29.2 %all-gather.13.cloned.1.call-start = ((), (), s32[]{:S(2)}) async-start(), calls=%async_computation.5 | async-start | bytes 2949120 | tf_op jit(solution)/shard_map/all_gather | solution.py:40
  7.9 84.6 %reduce-scatter.10.cloned.1.call-start = ((), (), s32[]{:S(2)}) async-start(), calls=%async_computation.10 | async-start | bytes 2949120 | tf_op jit(solution)/shard_map/reduce_scatter | solution.py:79
  44.6 1.7 copy-start.11
  44.7 97.8 %reduce-scatter.12.cloned.1.call-start = ((), (), s32[]{:S(2)}) async-start(), calls=%async_computation.12 | async-start | bytes 2949120 | tf_op jit(solution)/shard_map/reduce_scatter | solution.py:79
  53.7 138.1 %reduce-scatter.6.cloned.1.call-start = ((), (), s32[]{:S(2)}) async-start(), calls=%async_computation.6 | async-start | bytes 2949120 | tf_op jit(solution)/shard_map/reduce_scatter | solution.py:79
  61.2 179.8 %reduce-scatter.8.cloned.1.call-start = ((), (), s32[]{:S(2)}) async-start(), calls=%async_computation.8 | async-start | bytes 2949120 | tf_op jit(solution)/shard_map/reduce_scatter | solution.py:79
  68.7 172.4 %copy-start.9 = (bf16[192,6144]{1,0:T(8,128)(2,1)S(1)}, bf16[192,6144]{1,0:T(8,128)(2,1)}, u32[]{:S(2)}) copy-start(bf16[192,6144]{1,0:T(8,128)(2,1)} %param.8) | copy-start | bytes 7077892
  68.7 227.6 %all-gather.15.cloned.1.call-start = ((), (), s32[]{:S(2)}) async-start(), calls=%async_computation.7 | async-start | bytes 2949120 | tf_op jit(solution)/shard_map/all_gather | solution.py:87
  246.8 100.5 %all-gather.19.cloned.1.call-start = ((), (), s32[]{:S(2)}) async-start(), calls=%async_computation.11 | async-start | bytes 2949120 | tf_op jit(solution)/shard_map/all_gather | solution.py:87
  247.5 150.0 %all-gather.17.cloned.1.call-start = ((), (), s32[]{:S(2)}) async-start(), calls=%async_computation.9 | async-start | bytes 2949120 | tf_op jit(solution)/shard_map/all_gather | solution.py:87
  248.3 199.7 %all-gather.21.cloned.1.call-start = ((), (), s32[]{:S(2)}) async-start(), calls=%async_computation.13 | async-start | bytes 2949120 | tf_op jit(solution)/shard_map/all_gather | solution.py:87
  249.0 249.4 %all-gather.31.cloned.1.call-start = ((), (), s32[]{:S(2)}) async-start(), calls=%async_computation.19 | async-start | bytes 2949120 | tf_op jit(solution)/shard_map/all_gather | solution.py:85
  249.6 299.1 %all-gather.29.cloned.1.call-start = ((), (), s32[]{:S(2)}) async-start(), calls=%async_computation.18 | async-start | bytes 2949120 | tf_op jit(solution)/shard_map/all_gather | solution.py:85
  250.4 348.6 %all-gather.27.cloned.1.call-start = ((), (), s32[]{:S(2)}) async-start(), calls=%async_computation.17 | async-start | bytes 2949120 | tf_op jit(solution)/shard_map/all_gather | solution.py:85
  250.9 398.9 %all-gather.25.cloned.1.call-start = ((), (), s32[]{:S(2)}) async-start(), calls=%async_computation.16 | async-start | bytes 2949120 | tf_op jit(solution)/shard_map/all_gather | solution.py:85
  251.7 432.2 %reduce-scatter.14.cloned.1.call-start = ((), (), s32[]{:S(2)}) async-start(), calls=%async_computation.14 | async-start | bytes 2949120 | tf_op jit(solution)/shard_map/reduce_scatter | solution.py:97
  460.5 37.9 %copy-start.12 = (bf16[768,1536]{1,0:T(8,128)(2,1)S(1)}, bf16[768,1536]{1,0:T(8,128)(2,1)}, u32[]{:S(2)}) copy-start(bf16[768,1536]{1,0:T(8,128)(2,1)} %all-gather.13.cloned.1.call-done) | copy-start | bytes 7077892
  460.6 274.4 %all-gather.23.cloned.1.call-start = ((), (), s32[]{:S(2)}) async-start(), calls=%async_computation.15 | async-start | bytes 2949120 | tf_op jit(solution)/shard_map/all_gather | solution.py:47
  503.5 205.9 %collective-permute-start.7 = (bf16[1536,768]{1,0:T(8,128)(2,1)}, bf16[1536,768]{1,0:T(8,128)(2,1)}, u32[]{:S(2)}, u32[]{:S(2)}) collective-permute-start(bf16[1536,768]{1,0:T(8,128)(2,1)} %convolution_convert_fusion), channel_id=1, source_target_pairs={{0,16},{16,0},{1,17},{17,1},{2,18},{18,2},{3,19},{19,3},{4,20},{20... | collective-permute-start | bytes 7077896 | tf_op jit(solution)/shard_map/ppermute | solution.py:72
  553.9 163.1 %collective-permute-start.6 = (bf16[1536,768]{1,0:T(8,128)(2,1)}, bf16[1536,768]{1,0:T(8,128)(2,1)}, u32[]{:S(2)}, u32[]{:S(2)}) collective-permute-start(bf16[1536,768]{1,0:T(8,128)(2,1)} %convolution_convert_fusion.1), channel_id=1, source_target_pairs={{0,16},{16,0},{1,17},{17,1},{2,18},{18,2},{3,19},{19,3},{4,20},{20... | collective-permute-start | bytes 7077896 | tf_op jit(solution)/shard_map/ppermute | solution.py:72
  604.1 79.7 %copy-start.10 = (f32[1536]{0:T(1024)S(1)}, f32[1536]{0:T(1024)}, u32[]{:S(2)}) copy-start(f32[1536]{0:T(1024)} %param.9) | copy-start | bytes 18436
  604.1 118.9 %collective-permute-start.5 = (bf16[1536,768]{1,0:T(8,128)(2,1)}, bf16[1536,768]{1,0:T(8,128)(2,1)}, u32[]{:S(2)}, u32[]{:S(2)}) collective-permute-start(bf16[1536,768]{1,0:T(8,128)(2,1)} %convolution_convert_fusion.2), channel_id=1, source_target_pairs={{0,16},{16,0},{1,17},{17,1},{2,18},{18,2},{3,19},{19,3},{4,20},{20... | collective-permute-start | bytes 7077896 | tf_op jit(solution)/shard_map/ppermute | solution.py:72
  655.0 74.1 %collective-permute-start.4 = (bf16[1536,768]{1,0:T(8,128)(2,1)}, bf16[1536,768]{1,0:T(8,128)(2,1)}, u32[]{:S(2)}, u32[]{:S(2)}) collective-permute-start(bf16[1536,768]{1,0:T(8,128)(2,1)} %convolution_convert_fusion.3), channel_id=1, source_target_pairs={{0,16},{16,0},{1,17},{17,1},{2,18},{18,2},{3,19},{19,3},{4,20},{20... | collective-permute-start | bytes 7077896 | tf_op jit(solution)/shard_map/ppermute | solution.py:72
  683.9 4.8 copy-start.2
  686.5 2.6 copy-start.6
  688.7 1.7 copy-start.3
  690.8 18.0 %collective-permute-start.8 = (f32[6144]{0:T(1024)S(1)}, f32[6144]{0:T(1024)S(1)}, u32[]{:S(2)}, u32[]{:S(2)}) collective-permute-start(f32[6144]{0:T(1024)S(1)} %pad_maximum_fusion.2), channel_id=1, source_target_pairs={{0,16},{16,0},{1,17},{17,1},{2,18},{18,2},{3,19},{19,3},{4,20},{20... | collective-permute-start | bytes 73736 | tf_op jit(solution)/shard_map/ppermute | solution.py:94
  709.4 7.6 copy-start.13
  709.4 7.6 copy-start.14
  717.0 6.1 copy-start.15
  723.0 6.0 copy-start.16
  734.9 13.3 %slice-start = ((s8[4718592]{0:T(1024)(128)(4,1)}), s8[4194304]{0:T(1024)(128)(4,1)S(1)}, s32[]{:S(2)}) async-start(s8[4718592]{0:T(1024)(128)(4,1)} %bitcast.24), calls=%async_computation.20 | async-start | bytes 8388608
  734.9 13.3 %slice-start.2 = ((s8[4718592]{0:T(1024)(128)(4,1)}), s8[4194304]{0:T(1024)(128)(4,1)S(1)}, s32[]{:S(2)}) async-start(s8[4718592]{0:T(1024)(128)(4,1)} %bitcast.26), calls=%async_computation.22 | async-start | bytes 8388608
  734.9 13.3 %slice-start.4 = ((s8[4718592]{0:T(1024)(128)(4,1)}), s8[4194304]{0:T(1024)(128)(4,1)S(1)}, s32[]{:S(2)}) async-start(s8[4718592]{0:T(1024)(128)(4,1)} %bitcast.28), calls=%async_computation.24 | async-start | bytes 8388608
  740.5 7.7 slice-start.1
  740.5 7.7 slice-start.3
  740.6 7.7 slice-start.5
  740.6 175.8 %collective-permute-start = (bf16[768,1536]{1,0:T(8,128)(2,1)}, bf16[768,1536]{1,0:T(8,128)(2,1)}, u32[]{:S(2)}, u32[]{:S(2)}) collective-permute-start(bf16[768,1536]{1,0:T(8,128)(2,1)} %convolution_convert_fusion.7), channel_id=1, source_target_pairs={{0,16},{16,0},{1,17},{17,1},{2,18},{18,2},{3,19},{19,3},{4,20},{20... | collective-permute-start | bytes 7077896 | tf_op jit(solution)/shard_map/ppermute | solution.py:63
  742.1 6.2 copy-start.1
  747.7 7.5 copy-start.17
  747.7 172.6 %collective-permute-start.1 = (bf16[768,1536]{1,0:T(8,128)(2,1)}, bf16[768,1536]{1,0:T(8,128)(2,1)}, u32[]{:S(2)}, u32[]{:S(2)}) collective-permute-start(bf16[768,1536]{1,0:T(8,128)(2,1)} %convolution_convert_fusion.6), channel_id=1, source_target_pairs={{0,16},{16,0},{1,17},{17,1},{2,18},{18,2},{3,19},{19,3},{4,20},{20... | collective-permute-start | bytes 7077896 | tf_op jit(solution)/shard_map/ppermute | solution.py:63
  758.7 165.4 %collective-permute-start.2 = (bf16[768,1536]{1,0:T(8,128)(2,1)}, bf16[768,1536]{1,0:T(8,128)(2,1)}, u32[]{:S(2)}, u32[]{:S(2)}) collective-permute-start(bf16[768,1536]{1,0:T(8,128)(2,1)} %convolution_convert_fusion.5), channel_id=1, source_target_pairs={{0,16},{16,0},{1,17},{17,1},{2,18},{18,2},{3,19},{19,3},{4,20},{20... | collective-permute-start | bytes 7077896 | tf_op jit(solution)/shard_map/ppermute | solution.py:63
  909.2 5.7 copy-start.8
  909.2 7.2 copy-start.18
  913.4 3.0 copy-start.4
  913.4 51.5 %collective-permute-start.3 = (bf16[768,1536]{1,0:T(8,128)(2,1)S(1)}, bf16[768,1536]{1,0:T(8,128)(2,1)S(1)}, u32[]{:S(2)}, u32[]{:S(2)}) collective-permute-start(bf16[768,1536]{1,0:T(8,128)(2,1)S(1)} %convolution_convert_fusion.4), channel_id=1, source_target_pairs={{0,16},{16,0},{1,17},{17,1},{2,18},{18,2},{3,19},{19,3},{4,20},{20... | collective-permute-start | bytes 7077896 | tf_op jit(solution)/shard_map/ppermute | solution.py:63
  916.4 4.0 copy-start.7
  924.2 40.8 %copy-start.5 = (bf16[768,1536]{1,0:T(8,128)(2,1)S(1)}, bf16[768,1536]{1,0:T(8,128)(2,1)}, u32[]{:S(2)}) copy-start(bf16[768,1536]{1,0:T(8,128)(2,1)} %all-gather.21.cloned.1.call-done) | copy-start | bytes 7077892
  (1 other events, 1.1 us)
Sparse Core Ops, SparseCore 0:
  9.5 26.7 all-gather.12
  44.8 47.6 reduce-scatter.9
  95.4 47.0 reduce-scatter.11
  144.7 47.1 reduce-scatter.5
  194.0 47.0 reduce-scatter.7
  246.9 49.3 all-gather.14
  298.5 48.7 all-gather.18
  348.8 48.7 all-gather.16
  399.2 48.7 all-gather.20
  449.4 48.9 all-gather.30
  500.0 48.7 all-gather.28
  550.2 48.7 all-gather.26
  601.1 48.7 all-gather.24
  652.3 31.5 reduce-scatter.13
  686.6 24.0 all-gather.22
